TPU v7x, 256 devices: a whole 4x4x8 slice. The times are simulated.
256 devices in a mesh: seq: 8 (over x, core), dp: 8 (over z), fsdp: 4 (over y).
Axes of the slice: x: 4, y: 4, z: 8, core: 2. Of those that a mesh axis runs over, the one named last changes fastest.
Arguments:
- query_rows: bfloat16 [32, 1024, 4096], P(('dp', 'fsdp'), 'seq'), may hold values from -2.5 to 2.5
- forward_key_rows: bfloat16 [32, 1024, 1024], P(('dp', 'fsdp'), 'seq'), may hold values from -2.5 to 2.5
- forward_value_rows: bfloat16 [32, 1024, 1024], P(('dp', 'fsdp'), 'seq'), may hold values from -4 to 4
- out_cotangent: bfloat16 [32, 1024, 4096], P(('dp', 'fsdp'), 'seq'), may hold values from -12 to 12
- proj_weight: bfloat16 [4096, 4096], P(('dp', 'fsdp'), 'seq'), may hold values from -0.09375 to 0.09375
- sent_lengths: int32 [32, 32], P(('dp', 'fsdp')), may hold values from 1 to 64, 1024 in all within a row
Outputs:
- query_grad: bfloat16 [32, 1024, 4096], P(('dp', 'fsdp'), 'seq')
- key_gradient: bfloat16 [32, 1024, 1024], P(('dp', 'fsdp'), 'seq')
- value_gradient: bfloat16 [32, 1024, 1024], P(('dp', 'fsdp'), 'seq')
- proj_grad: bfloat16 [4096, 4096], P(('dp', 'fsdp'), 'seq')
Inputs may be any that keep to these rules, and one draw needn't show every extreme that they name: `sent_lengths`: each window's 32 lengths sum to 1024, and the longest is exactly 64.
All inputs are finite; a program needn't handle non-finite values.
Results may differ from a plain program's by a relative error of at most 0.0058.
Values may be sent and summed in bfloat16 or wider, within the bound.
No kernel may reach another device: no remote copies, remote signals or barrier semaphores. Data moves between devices by JAX's collectives and lax.ppermute only.
A program may use at most 128 MiB of HBM per device.

v0:
```python
import math
import jax
import jax.numpy as jnp
from jax import lax
from jax.sharding import PartitionSpec as P

QUERY_HEADS = 32
KEY_VALUE_HEADS = 8
HEAD_SIZE = 128


def per_device(
    query_rows, forward_key_rows, forward_value_rows, out_cotangent, proj_weight, sent_lengths
):
    queries_per_group = QUERY_HEADS // KEY_VALUE_HEADS
    factor = 1.0 / math.sqrt(HEAD_SIZE)
    gathered = lax.all_gather(out_cotangent, "seq", axis=1, tiled=True)
    cotangent = gathered[0]
    length = cotangent.shape[0]
    sliced = cotangent
    upstream_gradient = jnp.dot(
        sliced,
        lax.all_gather(proj_weight, ("dp", "fsdp"), axis=0, tiled=True),
        preferred_element_type=jnp.float32,
    ).astype(jnp.bfloat16)
    heads_of_queries, heads_of_keys, heads_of_values = (
        lax.all_to_all(query_rows, "seq", split_axis=2, concat_axis=1, tiled=True),
        lax.all_to_all(forward_key_rows, "seq", split_axis=2, concat_axis=1, tiled=True),
        lax.all_to_all(forward_value_rows, "seq", split_axis=2, concat_axis=1, tiled=True),
    )
    heads_of_queries = heads_of_queries[0]
    heads_of_keys = heads_of_keys[0]
    heads_of_values = heads_of_values[0]
    bounds = jnp.cumsum(sent_lengths[0])
    places = jnp.arange(length, dtype=jnp.int32)
    sentence = jnp.sum((places[:, None] >= bounds[None, :]).astype(jnp.int32), axis=1)
    block_rows = min(512, length)
    block_count = length // block_rows
    group_cols = queries_per_group * HEAD_SIZE
    key_head = heads_of_keys
    value_head = heads_of_values
    query_group = heads_of_queries

    def block_step(block_index, buffers):
        output_buf, query_buf, key_buf, value_buf = buffers
        offset = block_index * block_rows
        query_block = lax.dynamic_slice_in_dim(query_group, offset, block_rows, 0).reshape(
            block_rows, queries_per_group, HEAD_SIZE
        )
        upstream_block = lax.dynamic_slice_in_dim(upstream_gradient, offset, block_rows, 0).reshape(
            block_rows, queries_per_group, HEAD_SIZE
        )
        sentence_query = lax.dynamic_slice_in_dim(sentence, offset, block_rows, 0)
        allowed = (sentence[None, :] <= sentence_query[:, None]) & (
            sentence[None, :] >= sentence_query[:, None] - 3
        )
        scores = (
            jnp.einsum("qhd,kd->hqk", query_block, key_head, preferred_element_type=jnp.float32)
            * factor
        )
        raised = jnp.where(allowed[None], jnp.exp(scores), 0.0)
        attend = raised / jnp.sum(raised, axis=-1, keepdims=True)
        rounded = attend.astype(jnp.bfloat16)
        output_block = jnp.einsum(
            "hqk,kd->qhd", rounded, value_head, preferred_element_type=jnp.float32
        ).astype(jnp.bfloat16)
        grad_attend = jnp.einsum(
            "qhd,kd->hqk", upstream_block, value_head, preferred_element_type=jnp.float32
        )
        dscore = (
            attend * (grad_attend - jnp.sum(attend * grad_attend, axis=-1, keepdims=True)) * factor
        ).astype(jnp.bfloat16)
        query_block_grad = jnp.einsum(
            "hqk,kd->qhd", dscore, key_head, preferred_element_type=jnp.float32
        ).astype(jnp.bfloat16)
        key_window_grad = jnp.einsum(
            "hqk,qhd->kd", dscore, query_block, preferred_element_type=jnp.float32
        )
        value_window_grad = jnp.einsum(
            "hqk,qhd->kd", rounded, upstream_block, preferred_element_type=jnp.float32
        )
        output_buf = lax.dynamic_update_slice_in_dim(
            output_buf, output_block.reshape(block_rows, group_cols), offset, 0
        )
        query_buf = lax.dynamic_update_slice_in_dim(
            query_buf, query_block_grad.reshape(block_rows, group_cols), offset, 0
        )
        key_old = key_buf
        key_buf = key_old + key_window_grad
        value_old = value_buf
        value_buf = value_old + value_window_grad
        return (output_buf, query_buf, key_buf, value_buf)

    starting = (
        jnp.zeros((length, group_cols), jnp.bfloat16),
        jnp.zeros((length, group_cols), jnp.bfloat16),
        jnp.zeros((length, HEAD_SIZE), jnp.float32),
        jnp.zeros((length, HEAD_SIZE), jnp.float32),
    )
    output_buf, query_buf, key_buf, value_buf = lax.fori_loop(0, block_count, block_step, starting)
    key_parts = key_buf.astype(jnp.bfloat16)
    value_parts = value_buf.astype(jnp.bfloat16)
    sliced = cotangent
    proj_grad = lax.psum_scatter(
        lax.dot_general(
            sliced, output_buf, (((0,), (0,)), ((), ())), preferred_element_type=jnp.float32
        ),
        ("dp", "fsdp"),
        scatter_dimension=0,
        tiled=True,
    ).astype(jnp.bfloat16)
    query_grad, key_gradient, value_gradient = (
        lax.all_to_all(query_buf[None], "seq", split_axis=1, concat_axis=2, tiled=True),
        lax.all_to_all(key_parts[None], "seq", split_axis=1, concat_axis=2, tiled=True),
        lax.all_to_all(value_parts[None], "seq", split_axis=1, concat_axis=2, tiled=True),
    )
    return (query_grad, key_gradient, value_gradient, proj_grad)


def solution(mesh):
    in_specs = (
        P(("dp", "fsdp"), "seq", None),
        P(("dp", "fsdp"), "seq", None),
        P(("dp", "fsdp"), "seq", None),
        P(("dp", "fsdp"), "seq", None),
        P(("dp", "fsdp"), "seq"),
        P(("dp", "fsdp"), None),
    )
    out_specs = (
        P(("dp", "fsdp"), "seq", None),
        P(("dp", "fsdp"), "seq", None),
        P(("dp", "fsdp"), "seq", None),
        P(("dp", "fsdp"), "seq"),
    )
    return jax.shard_map(
        per_device, mesh=mesh, in_specs=in_specs, out_specs=out_specs, check_vma=False
    )
```

profile of v0, /device:TPU:2, one launch (start us, length us, event | category | flops | bytes accessed | tf_op | source)
XLA Modules:
  0.0 523.4 jit_solution(18148174244381852680)
XLA Ops:
  8.7 1.3 copy.118
  10.5 2.2 reduce.2
  13.5 5.6 %all-to-all-start.1 = ((bf16[8,2,8192]{2,1,0:T(2,128)(2,1)}), bf16[8,2,8192]{2,1,0:T(2,128)(2,1)S(1)}, u32[]{:S(2)}, u32[]{:S(2)}) async-start(bf16[8,2,8192]{2,1,0:T(2,128)(2,1)} %reshape.146), calls=%async_computation.1 | async-start | bytes 524288 | tf_op jit(solution)/shard_map/all_to_all | solution.py:28
  19.1 1.3 copy.120
  20.4 2.2 reduce.3
  23.4 1.8 all-to-all-done.1
  25.2 5.4 %all-to-all-start.2 = ((bf16[8,2,8192]{2,1,0:T(2,128)(2,1)}), bf16[8,2,8192]{2,1,0:T(2,128)(2,1)}, u32[]{:S(2)}, u32[]{:S(2)}) async-start(bf16[8,2,8192]{2,1,0:T(2,128)(2,1)} %reshape.148), calls=%async_computation.2 | async-start | bytes 524288 | tf_op jit(solution)/shard_map/all_to_all | solution.py:29
  30.5 5.0 copy.116
  35.6 22.4 %reduce.1 = bf16[4096,128]{1,0:T(8,128)(2,1)S(1)} reduce(bf16[4096,1,128]{2,1,0:T(2,128)(2,1)S(1)} %bitcast.213, bf16[]{:T(256)} %broadcast.149), dimensions={1}, to_apply=%bitcast.128.reduce_sub_computation | reduce | bytes 2097154
  58.0 1.1 reshape.144
  59.1 4.8 all-to-all-start
  63.9 13.1 %reduce-scatter.2.cloned.1.call-start = ((), (), s32[]{:S(2)}) async-start(), calls=%async_computation.9 | async-start | bytes 8650752 | tf_op jit(solution)/shard_map/reduce_scatter | solution.py:104
  78.8 1.2 reshape.149
  81.2 1.1 copy.150
  82.4 1.5 copy.117
  83.9 11.5 %all-gather.5.cloned.1.call-done = bf16[4096,512]{1,0:T(8,128)(2,1)} async-done(((bf16[128,512]{1,0:T(8,128)(2,1)}), bf16[4096,512]{1,0:T(8,128)(2,1)}) %all-gather.5.cloned.1.call-update) | async-done | bytes 4194320 | tf_op jit(solution)/shard_map/all_gather | solution.py:23
  95.4 50.1 %all-gather.3.cloned.1.call-done = bf16[1,1024,4096]{2,1,0:T(8,128)(2,1)} async-done(((bf16[1,128,4096]{2,1,0:T(8,128)(2,1)}), bf16[1,1024,4096]{2,1,0:T(8,128)(2,1)}) %all-gather.3.cloned.1.call-update) | async-done | bytes 8388624 | tf_op jit(solution)/shard_map/all_gather | solution.py:17
  145.5 10.1 %fusion.40 = bf16[1024,512]{1,0:T(8,128)(2,1)} fusion(bf16[4096,512]{1,0:T(8,128)(2,1)} %all-gather.5.cloned.1.call-done, bf16[1,1024,4096]{2,1,0:T(8,128)(2,1)} %all-gather.3.cloned.1.call-done), kind=kOutput, calls=%fused_computation.43 | convolution fusion | flops 4295491584 | bytes 13631488 | tf_op jit(solution)/shard_map/dot_general | solution.py:21
  155.6 1.1 broadcast.95.clone
  157.8 112.1 %while.22 = (s32[]{:T(128)}, bf16[1024,512]{0,1:T(8,128)(2,1)}, bf16[1024,512]{0,1:T(8,128)(2,1)}, f32[1024,128]{1,0:T(8,128)}, f32[1024,128]{1,0:T(8,128)}, /*i...) while((s32[]{:T(128)}, bf16[1024,512]{0,1:T(8,128)(2,1)}, ...), condition=%wide.region_5.6_spmd.clone, body=%wide.region_2.5_spmd.clone.sunk | while | flops 3293057536 | bytes 138467776 | solution.py:100
  160.0 4.5 fusion.72
  164.5 2.3 bitcast_reduce_fusion.2
  166.7 3.2 copy-done.11
  170.0 2.5 fusion.76
  172.5 17.1 %fusion.75 = f32[1024,128]{1,0:T(8,128)} fusion(bf16[512,4,128]{0,2,1:T(8,128)(2,1)S(1)} %bitcast.207, f32[512,4,1024]{2,0,1:T(8,128)} %fusion.72, f32[1024,128]{1,0:T(8,128)} %get-tuple-element.478, pred[]{:T(512)S(6)} %compare.3, f32[512,4,1024]{2,0,1:T(8,128)} %copy-done.11, f32[4,512]{1,0:T(4,128)S(1)} %get-tuple-element.458, ...), kind=kOutput, calls=%fused_computation.21.clone.1 | convolution fusion | flops 560204800 | bytes 18882560 | tf_op jit(solution)/shard_map/while/body/eval_jaxpr/hqk,qhd->kd/dot_general | solution.py:76
  189.6 16.9 %fusion.73 = bf16[4,512,128]{1,2,0:T(8,128)(2,1)S(1)} fusion(f32[512,4,1024]{2,0,1:T(8,128)} %fusion.72, bf16[1024,128]{0,1:T(8,128)(2,1)} %get-tuple-element.496, f32[512,4,1024]{2,0,1:T(8,128)} %copy-done.11, f32[4,512]{1,0:T(4,128)S(1)} %get-tuple-element.458, pred[512,1024]{1,0:T(8,128)(4,1)S(1)} %compare_and_fusion.2), kind=kOutput, calls=%fused_computation.18.clone.1 | convolution fusion | flops 560204800 | bytes 18096128 | tf_op jit(solution)/shard_map/while/body/eval_jaxpr/hqk,kd->qhd/dot_general | solution.py:73
  206.5 5.8 %fusion.74 = bf16[4,512,128]{1,2,0:T(8,128)(2,1)S(1)} fusion(bf16[1024,128]{1,0:T(8,128)(2,1)S(1)} %get-tuple-element.497, f32[512,4,1024]{2,0,1:T(8,128)} %copy-done.11, f32[4,512]{1,0:T(4,128)S(1)} %get-tuple-element.458, pred[512,1024]{1,0:T(8,128)(4,1)S(1)} %compare_and_fusion.2), kind=kOutput, calls=%fused_computation.17.clone.1 | convolution fusion | flops 545521664 | bytes 9707520 | tf_op jit(solution)/shard_map/while/body/eval_jaxpr/hqk,kd->qhd/dot_general | solution.py:64
  216.0 4.5 fusion.72
  220.5 2.3 bitcast_reduce_fusion.2
  222.8 3.2 copy-done.11
  226.0 2.5 fusion.76
  228.5 17.1 %fusion.75 = f32[1024,128]{1,0:T(8,128)} fusion(bf16[512,4,128]{0,2,1:T(8,128)(2,1)S(1)} %bitcast.207, f32[512,4,1024]{2,0,1:T(8,128)} %fusion.72, f32[1024,128]{1,0:T(8,128)} %get-tuple-element.478, pred[]{:T(512)S(6)} %compare.3, f32[512,4,1024]{2,0,1:T(8,128)} %copy-done.11, f32[4,512]{1,0:T(4,128)S(1)} %get-tuple-element.458, ...), kind=kOutput, calls=%fused_computation.21.clone.1 | convolution fusion | flops 560204800 | bytes 18882560 | tf_op jit(solution)/shard_map/while/body/eval_jaxpr/hqk,qhd->kd/dot_general | solution.py:76
  245.6 16.9 %fusion.73 = bf16[4,512,128]{1,2,0:T(8,128)(2,1)S(1)} fusion(f32[512,4,1024]{2,0,1:T(8,128)} %fusion.72, bf16[1024,128]{0,1:T(8,128)(2,1)} %get-tuple-element.496, f32[512,4,1024]{2,0,1:T(8,128)} %copy-done.11, f32[4,512]{1,0:T(4,128)S(1)} %get-tuple-element.458, pred[512,1024]{1,0:T(8,128)(4,1)S(1)} %compare_and_fusion.2), kind=kOutput, calls=%fused_computation.18.clone.1 | convolution fusion | flops 560204800 | bytes 18096128 | tf_op jit(solution)/shard_map/while/body/eval_jaxpr/hqk,kd->qhd/dot_general | solution.py:73
  262.6 5.8 %fusion.74 = bf16[4,512,128]{1,2,0:T(8,128)(2,1)S(1)} fusion(bf16[1024,128]{1,0:T(8,128)(2,1)S(1)} %get-tuple-element.497, f32[512,4,1024]{2,0,1:T(8,128)} %copy-done.11, f32[4,512]{1,0:T(4,128)S(1)} %get-tuple-element.458, pred[512,1024]{1,0:T(8,128)(4,1)S(1)} %compare_and_fusion.2), kind=kOutput, calls=%fused_computation.17.clone.1 | convolution fusion | flops 545521664 | bytes 9707520 | tf_op jit(solution)/shard_map/while/body/eval_jaxpr/hqk,kd->qhd/dot_general | solution.py:64
  269.9 11.4 %fusion.37 = f32[4096,512]{0,1:T(8,128)} fusion(bf16[1024,512]{0,1:T(8,128)(2,1)} %get-tuple-element.252, bf16[1,1024,4096]{2,1,0:T(8,128)(2,1)} %all-gather.3.cloned.1.call-done), kind=kOutput, calls=%fused_computation.42 | convolution fusion | flops 4294967296 | bytes 17825792 | tf_op jit(solution)/shard_map/dot_general | solution.py:105
  283.0 2.2 reduce.6
  286.0 4.7 all-to-all-start.5
  291.1 2.2 reduce.5
  294.1 2.7 all-to-all-done.5
  296.8 5.6 %all-to-all-start.4 = ((bf16[8,2,8192]{2,1,0:T(2,128)(2,1)}), bf16[8,2,8192]{2,1,0:T(2,128)(2,1)}, u32[]{:S(2)}, u32[]{:S(2)}) async-start(bf16[8,2,8192]{2,1,0:T(2,128)(2,1)} %reshape.152), calls=%async_computation.4 | async-start | bytes 524288 | tf_op jit(solution)/shard_map/all_to_all | solution.py:114
  302.4 1.8 copy.126
  304.3 7.1 %reduce.4 = bf16[1024,512]{1,0:T(8,128)(2,1)S(1)} reduce(bf16[1024,1,512]{2,1,0:T(2,128)(2,1)S(1)} %bitcast.212, bf16[]{:T(256)} %broadcast.149), dimensions={1}, to_apply=%bitcast.134.reduce_sub_computation | reduce | bytes 2097154
  311.3 1.6 reshape.150
  312.9 4.8 all-to-all-start.3
  319.1 1.2 reshape.153
  321.4 10.9 %all-to-all-done.3 = bf16[8,2,32768]{2,1,0:T(2,128)(2,1)S(1)} async-done(((bf16[8,2,32768]{2,1,0:T(2,128)(2,1)}), bf16[8,2,32768]{2,1,0:T(2,128)(2,1)S(1)}, u32[]{:S(2)}, u32[]{:S(2)}) %all-to-all-start.3) | async-done | bytes 1048608 | tf_op jit(solution)/shard_map/all_to_all | solution.py:113
  334.2 1.3 copy.132
  335.5 179.4 %reduce-scatter.2.cloned.1.call-done = f32[128,512]{0,1:T(8,128)} async-done(((f32[4096,512]{0,1:T(8,128)}), f32[128,512]{0,1:T(8,128)}) %reduce-scatter.2.cloned.1.call-update) | async-done | bytes 262160 | tf_op jit(solution)/shard_map/reduce_scatter | solution.py:104
  (94 shorter events, 24.6 us)
Async XLA Ops:
  7.2 88.2 %all-gather.5.cloned.1.call-start = ((), (), s32[]{:S(2)}) async-start(), calls=%async_computation.8 | async-start | bytes 4325376 | tf_op jit(solution)/shard_map/all_gather | solution.py:23
  7.9 69.1 %copy-start.10 = (s32[1,32]{1,0:T(1,128)S(1)}, s32[1,32]{1,0:T(1,128)}, u32[]{:S(2)}) copy-start(s32[1,32]{1,0:T(1,128)} %param.13) | copy-start | bytes 388
  7.9 137.6 %all-gather.3.cloned.1.call-start = ((), (), s32[]{:S(2)}) async-start(), calls=%async_computation.7 | async-start | bytes 9437184 | tf_op jit(solution)/shard_map/all_gather | solution.py:17
  13.5 11.6 %all-to-all-start.1 = ((bf16[8,2,8192]{2,1,0:T(2,128)(2,1)}), bf16[8,2,8192]{2,1,0:T(2,128)(2,1)S(1)}, u32[]{:S(2)}, u32[]{:S(2)}) async-start(bf16[8,2,8192]{2,1,0:T(2,128)(2,1)} %reshape.146), calls=%async_computation.1 | async-start | bytes 524288 | tf_op jit(solution)/shard_map/all_to_all | solution.py:28
  25.2 33.9 %all-to-all-start.2 = ((bf16[8,2,8192]{2,1,0:T(2,128)(2,1)}), bf16[8,2,8192]{2,1,0:T(2,128)(2,1)}, u32[]{:S(2)}, u32[]{:S(2)}) async-start(bf16[8,2,8192]{2,1,0:T(2,128)(2,1)} %reshape.148), calls=%async_computation.2 | async-start | bytes 524288 | tf_op jit(solution)/shard_map/all_to_all | solution.py:29
  59.1 21.1 %all-to-all-start = ((bf16[8,2,32768]{2,1,0:T(2,128)(2,1)}), bf16[8,2,32768]{2,1,0:T(2,128)(2,1)S(1)}, u32[]{:S(2)}, u32[]{:S(2)}) async-start(bf16[8,2,32768]{2,1,0:T(2,128)(2,1)} %reshape.144), calls=%async_computation | async-start | bytes 2097152 | tf_op jit(solution)/shard_map/all_to_all | solution.py:27
  63.9 451.0 %reduce-scatter.2.cloned.1.call-start = ((), (), s32[]{:S(2)}) async-start(), calls=%async_computation.9 | async-start | bytes 8650752 | tf_op jit(solution)/shard_map/reduce_scatter | solution.py:104
  159.9 4.5 copy-start.9
  159.9 10.0 %copy-start.5 = (f32[1024,128]{1,0:T(8,128)S(1)}, f32[1024,128]{1,0:T(8,128)}, u32[]{:S(2)}) copy-start(f32[1024,128]{1,0:T(8,128)} %get-tuple-element.479) | copy-start | bytes 1572868 | tf_op jit(solution)/shard_map/while
  166.7 3.2 copy-start.11
  172.5 17.1 %copy-start.6 = (f32[1024,128]{1,0:T(8,128)}, f32[1024,128]{1,0:T(8,128)S(1)}, u32[]{:S(2)}) copy-start(f32[1024,128]{1,0:T(8,128)S(1)} %fusion.76) | copy-start | bytes 1572868 | tf_op jit(solution)/shard_map/while
  206.5 5.8 %copy-start = (bf16[1024,512]{0,1:T(8,128)(2,1)S(1)}, bf16[1024,512]{0,1:T(8,128)(2,1)}, u32[]{:S(2)}) copy-start(bf16[1024,512]{0,1:T(8,128)(2,1)} %get-tuple-element.477) | copy-start | bytes 3145732 | tf_op jit(solution)/shard_map/while
  206.5 5.8 %copy-start.3 = (bf16[1024,512]{0,1:T(8,128)(2,1)S(1)}, bf16[1024,512]{0,1:T(8,128)(2,1)}, u32[]{:S(2)}) copy-start(bf16[1024,512]{0,1:T(8,128)(2,1)} %get-tuple-element.476) | copy-start | bytes 3145732 | tf_op jit(solution)/shard_map/while
  212.5 1.0 copy-start.1
  212.5 1.3 copy-start.4
  216.0 4.5 copy-start.9
  216.0 10.0 %copy-start.5 = (f32[1024,128]{1,0:T(8,128)S(1)}, f32[1024,128]{1,0:T(8,128)}, u32[]{:S(2)}) copy-start(f32[1024,128]{1,0:T(8,128)} %get-tuple-element.479) | copy-start | bytes 1572868 | tf_op jit(solution)/shard_map/while
  222.8 3.2 copy-start.11
  228.5 17.1 %copy-start.6 = (f32[1024,128]{1,0:T(8,128)}, f32[1024,128]{1,0:T(8,128)S(1)}, u32[]{:S(2)}) copy-start(f32[1024,128]{1,0:T(8,128)S(1)} %fusion.76) | copy-start | bytes 1572868 | tf_op jit(solution)/shard_map/while
  262.6 5.8 %copy-start = (bf16[1024,512]{0,1:T(8,128)(2,1)S(1)}, bf16[1024,512]{0,1:T(8,128)(2,1)}, u32[]{:S(2)}) copy-start(bf16[1024,512]{0,1:T(8,128)(2,1)} %get-tuple-element.477) | copy-start | bytes 3145732 | tf_op jit(solution)/shard_map/while
  262.6 5.8 %copy-start.3 = (bf16[1024,512]{0,1:T(8,128)(2,1)S(1)}, bf16[1024,512]{0,1:T(8,128)(2,1)}, u32[]{:S(2)}) copy-start(bf16[1024,512]{0,1:T(8,128)(2,1)} %get-tuple-element.476) | copy-start | bytes 3145732 | tf_op jit(solution)/shard_map/while
  268.6 1.0 copy-start.1
  268.6 1.3 copy-start.4
  281.3 1.0 copy-start.7
  281.3 1.2 copy-start.8
  281.3 21.1 %copy-start.2 = (bf16[1024,512]{0,1:T(8,128)(2,1)S(1)}, bf16[1024,512]{0,1:T(8,128)(2,1)}, u32[]{:S(2)}) copy-start(bf16[1024,512]{0,1:T(8,128)(2,1)} %get-tuple-element.249) | copy-start | bytes 3145732
  286.0 10.7 %all-to-all-start.5 = ((bf16[8,2,8192]{2,1,0:T(2,128)(2,1)}), bf16[8,2,8192]{2,1,0:T(2,128)(2,1)S(1)}, u32[]{:S(2)}, u32[]{:S(2)}) async-start(bf16[8,2,8192]{2,1,0:T(2,128)(2,1)} %reshape.154), calls=%async_computation.5 | async-start | bytes 524288 | tf_op jit(solution)/shard_map/all_to_all | solution.py:115
  296.8 16.2 %all-to-all-start.4 = ((bf16[8,2,8192]{2,1,0:T(2,128)(2,1)}), bf16[8,2,8192]{2,1,0:T(2,128)(2,1)}, u32[]{:S(2)}, u32[]{:S(2)}) async-start(bf16[8,2,8192]{2,1,0:T(2,128)(2,1)} %reshape.152), calls=%async_computation.4 | async-start | bytes 524288 | tf_op jit(solution)/shard_map/all_to_all | solution.py:114
  312.9 19.3 %all-to-all-start.3 = ((bf16[8,2,32768]{2,1,0:T(2,128)(2,1)}), bf16[8,2,32768]{2,1,0:T(2,128)(2,1)S(1)}, u32[]{:S(2)}, u32[]{:S(2)}) async-start(bf16[8,2,32768]{2,1,0:T(2,128)(2,1)} %reshape.150), calls=%async_computation.3 | async-start | bytes 2097152 | tf_op jit(solution)/shard_map/all_to_all | solution.py:113
Sparse Core Ops, SparseCore 0:
  10.6 84.7 all-gather.4
  97.2 48.1 all-gather.2
  281.5 233.3 reduce-scatter.1
where the time goes:
time: 531 us; the launch traced here: 523 us
  waiting for transfers between devices  258 us (49%)
  matrix products  120 us (23%)
  local copies, waits for them, and re-layouts  46.6 us (9%)
  starting transfers between devices  44 us (8%)
  other arithmetic  40.9 us (8%)
  between operations  14.3 us (3%)
    reduce_scatter x1, waiting for transfers between devices, per_device(): lax.psum_scatter(lax.dot_general(sliced, output_buf, (((0,), (0,)), ((),...  179 us
    all_gather x1, waiting for transfers between devices, per_device(): gathered = lax.all_gather(out_cotangent, 'seq', axis=1, tiled=True)  50.1 us
    unnamed x8, other arithmetic  38.5 us
    dot_general x2, matrix products, block_step(): jnp.einsum('hqk,qhd->kd', dscore, query_block, preferred_element_type=jnp...  34.2 us
    dot_general x2, matrix products, block_step(): jnp.einsum('hqk,kd->qhd', dscore, key_head, preferred_element_type=jnp.fl...  33.9 us
    unnamed x35, local copies, waits for them, and re-layouts  26.2 us
    reduce_scatter x1, starting transfers between devices, per_device(): lax.psum_scatter(lax.dot_general(sliced, output_buf, (((0,), (0,)), ((),...  13.1 us
    dot_general x2, matrix products, block_step(): jnp.einsum('hqk,kd->qhd', rounded, value_head, preferred_element_type=jnp...  11.5 us
  transfers between devices with their start and end apart: 9, of which 6 were waited for; matrix products, arithmetic and copies ran while one was open for 13% of the time, Pallas kernels for 0%

commit v1 on v0

--- a/solution.py
+++ b/solution.py
@@ -14,7 +14,9 @@
 ):
     queries_per_group = QUERY_HEADS // KEY_VALUE_HEADS
     factor = 1.0 / math.sqrt(HEAD_SIZE)
-    gathered = lax.all_gather(out_cotangent, "seq", axis=1, tiled=True)
+    gathered = jnp.concatenate(
+        lax.all_to_all(jnp.stack([out_cotangent] * lax.axis_size("seq")), "seq", 0, 0), axis=1
+    )
     cotangent = gathered[0]
     length = cotangent.shape[0]
     sliced = cotangent

time: 531 us -> 571 us (1.075)
  waiting for transfers between devices: 258 us -> 282 us
  local copies, waits for them, and re-layouts: 46.6 us -> 53.4 us
  starting transfers between devices: 44 us -> 50.5 us
    all_to_all x0 -> x1, waiting for transfers between devices: none -> 73.4 us  [per_device(): lax.all_to_all(jnp.stack([out_cotangent] * lax.axis_size('seq')), 'seq',...]
    all_gather x1 -> x0, waiting for transfers between devices: 50.1 us -> none  [per_device(): gathered = lax.all_gather(out_cotangent, 'seq', axis=1, tiled=True)]
    all_to_all x1, waiting for transfers between devices: 0.01 us -> 13.8 us  [per_device(): lax.all_to_all(query_rows, 'seq', split_axis=2, concat_axis=1, tiled=True)]
    all_gather x1, waiting for transfers between devices: 11.5 us -> 0.01 us  [per_device(): lax.all_gather(proj_weight, ('dp', 'fsdp'), axis=0, tiled=True)]
    all_to_all x0 -> x1, starting transfers between devices: none -> 6.44 us  [per_device(): lax.all_to_all(jnp.stack([out_cotangent] * lax.axis_size('seq')), 'seq',...]
    unnamed x35 -> x33, local copies, waits for them, and re-layouts: 26.2 us -> 26.1 us
  transfers between devices with their start and end apart: 9 -> 9, of which waited for: 6 -> 6; matrix products, arithmetic and copies ran while one was open for 13% -> 12% of each run, Pallas kernels for 0% -> 0%
where the time goes in v1:
time: 571 us; the launch traced here: 563 us
  waiting for transfers between devices  282 us (49%)
  matrix products  120 us (21%)
  local copies, waits for them, and re-layouts  53.4 us (9%)
  starting transfers between devices  50.5 us (9%)
  other arithmetic  41.9 us (7%)
  between operations  14.5 us (3%)
    reduce_scatter x1, waiting for transfers between devices, per_device(): lax.psum_scatter(lax.dot_general(sliced, output_buf, (((0,), (0,)), ((),...  179 us
    all_to_all x1, waiting for transfers between devices, per_device(): lax.all_to_all(jnp.stack([out_cotangent] * lax.axis_size('seq')), 'seq',...  73.4 us
    unnamed x8, other arithmetic  38.5 us
    dot_general x2, matrix products, block_step(): jnp.einsum('hqk,kd->qhd', dscore, key_head, preferred_element_type=jnp.fl...  33.8 us
    dot_general x2, matrix products, block_step(): jnp.einsum('hqk,qhd->kd', dscore, query_block, preferred_element_type=jnp...  32.2 us
    unnamed x33, local copies, waits for them, and re-layouts  26.1 us
    all_to_all x1, waiting for transfers between devices, per_device(): lax.all_to_all(query_rows, 'seq', split_axis=2, concat_axis=1, tiled=True)  13.8 us
    reduce_scatter x1, starting transfers between devices, per_device(): lax.psum_scatter(lax.dot_general(sliced, output_buf, (((0,), (0,)), ((),...  13 us
  transfers between devices with their start and end apart: 9, of which 6 were waited for; matrix products, arithmetic and copies ran while one was open for 12% of the time, Pallas kernels for 0%

profile of v1, /device:TPU:2, one launch (start us, length us, event | category | flops | bytes accessed | tf_op | source)
XLA Modules:
  0.0 562.7 jit_solution(15571753905118896288)
XLA Ops:
  7.2 1.3 copy.118
  9.0 2.2 reduce.2
  12.0 5.6 all-to-all-start.1
  17.6 1.3 copy.120
  18.9 2.2 reduce.3
  21.9 1.8 all-to-all-done.1
  23.7 5.4 all-to-all-start.2
  29.0 5.0 copy.116
  34.1 22.4 %reduce.1 = bf16[4096,128]{1,0:T(8,128)(2,1)S(1)} reduce(bf16[4096,1,128]{2,1,0:T(2,128)(2,1)S(1)} %bitcast.208, bf16[]{:T(256)} %broadcast.152), dimensions={1}, to_apply=%bitcast.121.reduce_sub_computation | reduce | bytes 2097154
  57.6 4.8 all-to-all-start
  63.2 13.8 %all-to-all-done = bf16[8,2,32768]{2,1,0:T(2,128)(2,1)S(1)} async-done(((bf16[8,2,32768]{2,1,0:T(2,128)(2,1)}), bf16[8,2,32768]{2,1,0:T(2,128)(2,1)S(1)}, u32[]{:S(2)}, u32[]{:S(2)}) %all-to-all-start) | async-done | bytes 1048608 | tf_op jit(solution)/shard_map/all_to_all | solution.py:29
  76.9 5.5 stack.2
  82.4 6.4 %all-to-all-start.3 = ((bf16[8,1,128,4096]{3,2,1,0:T(8,128)(2,1)}), bf16[8,1,128,4096]{3,2,1,0:T(8,128)(2,1)}, u32[]{:S(2)}, u32[]{:S(2)}) async-start(bf16[8,1,128,4096]{3,2,1,0:T(8,128)(2,1)} %stack.2), calls=%async_computation.3 | async-start | bytes 16777216 | tf_op jit(solution)/shard_map/all_to_all | solution.py:18
  88.8 13.0 %reduce-scatter.2.cloned.1.call-start = ((), (), s32[]{:S(2)}) async-start(), calls=%async_computation.9 | async-start | bytes 8650752 | tf_op jit(solution)/shard_map/reduce_scatter | solution.py:106
  103.6 1.2 reshape.152
  107.2 1.5 copy.117
  108.7 73.4 %all-to-all-done.3 = bf16[8,1,128,4096]{3,2,1,0:T(8,128)(2,1)} async-done(((bf16[8,1,128,4096]{3,2,1,0:T(8,128)(2,1)}), bf16[8,1,128,4096]{3,2,1,0:T(8,128)(2,1)}, u32[]{:S(2)}, u32[]{:S(2)}) %all-to-all-start.3) | async-done | bytes 8388640 | tf_op jit(solution)/shard_map/all_to_all | solution.py:18
  182.1 10.1 %convolution_convert_fusion = bf16[1024,512]{1,0:T(8,128)(2,1)} fusion(bf16[1024,4096]{1,0:T(8,128)(2,1)} %bitcast.8, bf16[4096,512]{1,0:T(8,128)(2,1)} %all-gather.2.cloned.1.call-done), kind=kOutput, calls=%fused_computation.39 | convolution fusion | flops 4295491584 | bytes 13631488 | tf_op jit(solution)/shard_map/dot_general | solution.py:23
  194.4 114.3 %while.22 = (s32[]{:T(128)}, bf16[1024,512]{0,1:T(8,128)(2,1)}, bf16[1024,512]{0,1:T(8,128)(2,1)}, f32[1024,128]{1,0:T(8,128)}, f32[1024,128]{1,0:T(8,128)}, /*i...) while((s32[]{:T(128)}, bf16[1024,512]{0,1:T(8,128)(2,1)}, ...), condition=%wide.region_5.6_spmd.clone, body=%wide.region_2.5_spmd.clone.sunk | while | flops 3293057536 | bytes 138467776 | solution.py:102
  196.6 4.5 fusion.64
  201.1 2.3 bitcast_reduce_fusion.2
  203.3 3.2 copy-done.10
  206.6 3.3 fusion.68
  209.8 16.1 %fusion.67 = f32[1024,128]{1,0:T(8,128)S(1)} fusion(bf16[512,4,128]{0,2,1:T(8,128)(2,1)S(1)} %bitcast.202, f32[512,4,1024]{2,0,1:T(8,128)} %fusion.64, f32[1024,128]{1,0:T(8,128)S(1)} %copy-done.5, pred[]{:T(512)S(6)} %compare.3, f32[512,4,1024]{2,0,1:T(8,128)} %copy-done.10, f32[4,512]{1,0:T(4,128)S(1)} %get-tuple-element.458, ...), kind=kOutput, calls=%fused_computation.21.clone.1 | convolution fusion | flops 560204800 | bytes 18882560 | tf_op jit(solution)/shard_map/while/body/eval_jaxpr/hqk,qhd->kd/dot_general | solution.py:78
  226.8 16.9 %fusion.65 = bf16[4,512,128]{1,2,0:T(8,128)(2,1)S(1)} fusion(f32[512,4,1024]{2,0,1:T(8,128)} %fusion.64, bf16[1024,128]{0,1:T(8,128)(2,1)} %get-tuple-element.496, f32[512,4,1024]{2,0,1:T(8,128)} %copy-done.10, f32[4,512]{1,0:T(4,128)S(1)} %get-tuple-element.458, pred[512,1024]{1,0:T(8,128)(4,1)S(1)} %compare_and_fusion.2), kind=kOutput, calls=%fused_computation.18.clone.1 | convolution fusion | flops 560204800 | bytes 18096128 | tf_op jit(solution)/shard_map/while/body/eval_jaxpr/hqk,kd->qhd/dot_general | solution.py:75
  243.7 5.8 %fusion.66 = bf16[4,512,128]{1,2,0:T(8,128)(2,1)S(1)} fusion(bf16[1024,128]{1,0:T(8,128)(2,1)S(1)} %get-tuple-element.497, f32[512,4,1024]{2,0,1:T(8,128)} %copy-done.10, f32[4,512]{1,0:T(4,128)S(1)} %get-tuple-element.458, pred[512,1024]{1,0:T(8,128)(4,1)S(1)} %compare_and_fusion.2), kind=kOutput, calls=%fused_computation.17.clone.1 | convolution fusion | flops 545521664 | bytes 9707520 | tf_op jit(solution)/shard_map/while/body/eval_jaxpr/hqk,kd->qhd/dot_general | solution.py:66
  253.1 4.5 fusion.64
  257.6 2.3 bitcast_reduce_fusion.2
  259.9 3.2 copy-done.10
  263.1 4.4 fusion.68
  267.5 16.1 %fusion.67 = f32[1024,128]{1,0:T(8,128)S(1)} fusion(bf16[512,4,128]{0,2,1:T(8,128)(2,1)S(1)} %bitcast.202, f32[512,4,1024]{2,0,1:T(8,128)} %fusion.64, f32[1024,128]{1,0:T(8,128)S(1)} %copy-done.5, pred[]{:T(512)S(6)} %compare.3, f32[512,4,1024]{2,0,1:T(8,128)} %copy-done.10, f32[4,512]{1,0:T(4,128)S(1)} %get-tuple-element.458, ...), kind=kOutput, calls=%fused_computation.21.clone.1 | convolution fusion | flops 560204800 | bytes 18882560 | tf_op jit(solution)/shard_map/while/body/eval_jaxpr/hqk,qhd->kd/dot_general | solution.py:78
  284.5 16.9 %fusion.65 = bf16[4,512,128]{1,2,0:T(8,128)(2,1)S(1)} fusion(f32[512,4,1024]{2,0,1:T(8,128)} %fusion.64, bf16[1024,128]{0,1:T(8,128)(2,1)} %get-tuple-element.496, f32[512,4,1024]{2,0,1:T(8,128)} %copy-done.10, f32[4,512]{1,0:T(4,128)S(1)} %get-tuple-element.458, pred[512,1024]{1,0:T(8,128)(4,1)S(1)} %compare_and_fusion.2), kind=kOutput, calls=%fused_computation.18.clone.1 | convolution fusion | flops 560204800 | bytes 18096128 | tf_op jit(solution)/shard_map/while/body/eval_jaxpr/hqk,kd->qhd/dot_general | solution.py:75
  301.4 5.8 %fusion.66 = bf16[4,512,128]{1,2,0:T(8,128)(2,1)S(1)} fusion(bf16[1024,128]{1,0:T(8,128)(2,1)S(1)} %get-tuple-element.497, f32[512,4,1024]{2,0,1:T(8,128)} %copy-done.10, f32[4,512]{1,0:T(4,128)S(1)} %get-tuple-element.458, pred[512,1024]{1,0:T(8,128)(4,1)S(1)} %compare_and_fusion.2), kind=kOutput, calls=%fused_computation.17.clone.1 | convolution fusion | flops 545521664 | bytes 9707520 | tf_op jit(solution)/shard_map/while/body/eval_jaxpr/hqk,kd->qhd/dot_general | solution.py:66
  308.7 11.4 %convolution_bitcast_fusion = f32[4096,512]{0,1:T(8,128)} fusion(bf16[1024,512]{0,1:T(8,128)(2,1)} %get-tuple-element.252, bf16[1024,4096]{1,0:T(8,128)(2,1)} %bitcast.8), kind=kOutput, calls=%fused_computation.38 | convolution fusion | flops 4294967296 | bytes 17825792 | tf_op jit(solution)/shard_map/dot_general | solution.py:107
  321.1 1.1 convert_bitcast_fusion
  322.7 2.2 reduce.6
  325.7 4.8 all-to-all-start.6
  330.9 2.2 reduce.5
  333.9 2.7 all-to-all-done.6
  336.6 5.6 %all-to-all-start.5 = ((bf16[8,2,8192]{2,1,0:T(2,128)(2,1)}), bf16[8,2,8192]{2,1,0:T(2,128)(2,1)}, u32[]{:S(2)}, u32[]{:S(2)}) async-start(bf16[8,2,8192]{2,1,0:T(2,128)(2,1)} %reshape.155), calls=%async_computation.5 | async-start | bytes 524288 | tf_op jit(solution)/shard_map/all_to_all | solution.py:116
  342.2 1.8 copy.126
  344.0 7.1 %reduce.4 = bf16[1024,512]{1,0:T(8,128)(2,1)S(1)} reduce(bf16[1024,1,512]{2,1,0:T(2,128)(2,1)S(1)} %bitcast.207, bf16[]{:T(256)} %broadcast.152), dimensions={1}, to_apply=%bitcast.127.reduce_sub_computation | reduce | bytes 2097154
  351.1 1.6 reshape.153
  352.7 4.8 all-to-all-start.4
  358.9 1.2 reshape.156
  361.2 10.9 %all-to-all-done.4 = bf16[8,2,32768]{2,1,0:T(2,128)(2,1)S(1)} async-done(((bf16[8,2,32768]{2,1,0:T(2,128)(2,1)}), bf16[8,2,32768]{2,1,0:T(2,128)(2,1)S(1)}, u32[]{:S(2)}, u32[]{:S(2)}) %all-to-all-start.4) | async-done | bytes 1048608 | tf_op jit(solution)/shard_map/all_to_all | solution.py:115
  374.0 1.3 copy.132
  375.3 178.6 %reduce-scatter.2.cloned.1.call-done = f32[128,512]{0,1:T(8,128)} async-done(((f32[4096,512]{0,1:T(8,128)}), f32[128,512]{0,1:T(8,128)}) %reduce-scatter.2.cloned.1.call-update) | async-done | bytes 262160 | tf_op jit(solution)/shard_map/reduce_scatter | solution.py:106
  (92 shorter events, 28.5 us)
Async XLA Ops:
  12.0 11.6 %all-to-all-start.1 = ((bf16[8,2,8192]{2,1,0:T(2,128)(2,1)}), bf16[8,2,8192]{2,1,0:T(2,128)(2,1)S(1)}, u32[]{:S(2)}, u32[]{:S(2)}) async-start(bf16[8,2,8192]{2,1,0:T(2,128)(2,1)} %reshape.149), calls=%async_computation.1 | async-start | bytes 524288 | tf_op jit(solution)/shard_map/all_to_all | solution.py:30
  23.7 33.9 %all-to-all-start.2 = ((bf16[8,2,8192]{2,1,0:T(2,128)(2,1)}), bf16[8,2,8192]{2,1,0:T(2,128)(2,1)}, u32[]{:S(2)}, u32[]{:S(2)}) async-start(bf16[8,2,8192]{2,1,0:T(2,128)(2,1)} %reshape.151), calls=%async_computation.2 | async-start | bytes 524288 | tf_op jit(solution)/shard_map/all_to_all | solution.py:31
  57.6 19.3 %all-to-all-start = ((bf16[8,2,32768]{2,1,0:T(2,128)(2,1)}), bf16[8,2,32768]{2,1,0:T(2,128)(2,1)S(1)}, u32[]{:S(2)}, u32[]{:S(2)}) async-start(bf16[8,2,32768]{2,1,0:T(2,128)(2,1)} %reshape.147), calls=%async_computation | async-start | bytes 2097152 | tf_op jit(solution)/shard_map/all_to_all | solution.py:29
  62.4 119.7 %all-gather.2.cloned.1.call-start = ((), (), s32[]{:S(2)}) async-start(), calls=%async_computation.8 | async-start | bytes 4325376 | tf_op jit(solution)/shard_map/all_gather | solution.py:25
  82.4 19.5 %copy-start.9 = (s32[1,32]{1,0:T(1,128)S(1)}, s32[1,32]{1,0:T(1,128)}, u32[]{:S(2)}) copy-start(s32[1,32]{1,0:T(1,128)} %param.13) | copy-start | bytes 388
  82.4 99.7 %all-to-all-start.3 = ((bf16[8,1,128,4096]{3,2,1,0:T(8,128)(2,1)}), bf16[8,1,128,4096]{3,2,1,0:T(8,128)(2,1)}, u32[]{:S(2)}, u32[]{:S(2)}) async-start(bf16[8,1,128,4096]{3,2,1,0:T(8,128)(2,1)} %stack.2), calls=%async_computation.3 | async-start | bytes 16777216 | tf_op jit(solution)/shard_map/all_to_all | solution.py:18
  88.8 465.1 %reduce-scatter.2.cloned.1.call-start = ((), (), s32[]{:S(2)}) async-start(), calls=%async_computation.9 | async-start | bytes 8650752 | tf_op jit(solution)/shard_map/reduce_scatter | solution.py:106
  196.6 4.5 copy-start.8
  203.3 3.2 copy-start.10
  206.6 3.3 copy-start.5
  226.0 0.8 copy-start.6
  243.7 5.8 %copy-start = (bf16[1024,512]{0,1:T(8,128)(2,1)S(1)}, bf16[1024,512]{0,1:T(8,128)(2,1)}, u32[]{:S(2)}) copy-start(bf16[1024,512]{0,1:T(8,128)(2,1)} %get-tuple-element.477) | copy-start | bytes 3145732 | tf_op jit(solution)/shard_map/while
  243.7 5.8 %copy-start.3 = (bf16[1024,512]{0,1:T(8,128)(2,1)S(1)}, bf16[1024,512]{0,1:T(8,128)(2,1)}, u32[]{:S(2)}) copy-start(bf16[1024,512]{0,1:T(8,128)(2,1)} %get-tuple-element.476) | copy-start | bytes 3145732 | tf_op jit(solution)/shard_map/while
  249.7 1.0 copy-start.1
  249.7 1.3 copy-start.4
  253.1 4.5 copy-start.8
  259.9 3.2 copy-start.10
  263.1 4.4 copy-start.5
  283.6 0.8 copy-start.6
  301.4 5.8 %copy-start = (bf16[1024,512]{0,1:T(8,128)(2,1)S(1)}, bf16[1024,512]{0,1:T(8,128)(2,1)}, u32[]{:S(2)}) copy-start(bf16[1024,512]{0,1:T(8,128)(2,1)} %get-tuple-element.477) | copy-start | bytes 3145732 | tf_op jit(solution)/shard_map/while
  301.4 5.8 %copy-start.3 = (bf16[1024,512]{0,1:T(8,128)(2,1)S(1)}, bf16[1024,512]{0,1:T(8,128)(2,1)}, u32[]{:S(2)}) copy-start(bf16[1024,512]{0,1:T(8,128)(2,1)} %get-tuple-element.476) | copy-start | bytes 3145732 | tf_op jit(solution)/shard_map/while
  307.4 1.0 copy-start.1
  307.4 1.3 copy-start.4
  320.1 1.0 copy-start.7
  320.1 22.1 %copy-start.2 = (bf16[1024,512]{0,1:T(8,128)(2,1)S(1)}, bf16[1024,512]{0,1:T(8,128)(2,1)}, u32[]{:S(2)}) copy-start(bf16[1024,512]{0,1:T(8,128)(2,1)} %get-tuple-element.249) | copy-start | bytes 3145732
  325.7 10.9 %all-to-all-start.6 = ((bf16[8,2,8192]{2,1,0:T(2,128)(2,1)}), bf16[8,2,8192]{2,1,0:T(2,128)(2,1)S(1)}, u32[]{:S(2)}, u32[]{:S(2)}) async-start(bf16[8,2,8192]{2,1,0:T(2,128)(2,1)} %reshape.157), calls=%async_computation.6 | async-start | bytes 524288 | tf_op jit(solution)/shard_map/all_to_all | solution.py:117
  336.6 16.2 %all-to-all-start.5 = ((bf16[8,2,8192]{2,1,0:T(2,128)(2,1)}), bf16[8,2,8192]{2,1,0:T(2,128)(2,1)}, u32[]{:S(2)}, u32[]{:S(2)}) async-start(bf16[8,2,8192]{2,1,0:T(2,128)(2,1)} %reshape.155), calls=%async_computation.5 | async-start | bytes 524288 | tf_op jit(solution)/shard_map/all_to_all | solution.py:116
  352.7 19.3 %all-to-all-start.4 = ((bf16[8,2,32768]{2,1,0:T(2,128)(2,1)}), bf16[8,2,32768]{2,1,0:T(2,128)(2,1)S(1)}, u32[]{:S(2)}, u32[]{:S(2)}) async-start(bf16[8,2,32768]{2,1,0:T(2,128)(2,1)} %reshape.153), calls=%async_computation.4 | async-start | bytes 2097152 | tf_op jit(solution)/shard_map/all_to_all | solution.py:115
Sparse Core Ops, SparseCore 0:
  65.8 83.9 all-gather.1
  320.3 233.5 reduce-scatter.1
